TPU v7x, 256 devices: a whole 4x4x8 slice. The times are simulated.
256 devices in a mesh: row: 4 (over x_lo, core), col: 64 (over y, x_hi, z).
Axes of the slice: x: 4 (x_hi: 2, x_lo: 2; x = x_hi * 2 + x_lo), y: 4, z: 8, core: 2. Of those that a mesh axis runs over, the one named last changes fastest.
Arguments:
- test_points: float32 [3, 4096], P(None, ('row', 'col')), may hold values from 0 to 1
- src_points: float32 [3, 262144], P(None, ('row', 'col')), may hold values from 0 to 1
- currents: float32 [2, 262144], P(None, ('row', 'col')), may hold values from -6 to 6
- near_blocks: float32 [16384, 2, 16, 128], P(('row', 'col')), may hold values from -0.3 to 0.3
- near_dest: int32 [16384, 1], P(('row', 'col')), may hold values from 0 to 63; in each aligned block of 64 rows (0 to 63, 64 to 127, ...) at most 2 rows name the same one
- near_tile: int32 [16384, 1], P(('row', 'col')), may hold values from 0 to 7
Outputs:
- field: float32 [2, 4096], P(None, ('row', 'col'))
Inputs may be any that keep to these rules, and one draw needn't show every extreme that they name: `near_dest`: among the 64 blocks held by one device, at most 2 name the same column index; some device reaches 2 in every draw.
All inputs are finite; a program needn't handle non-finite values.
Results may differ from a plain program's by a relative error of at most 0.0003.
Values sent between devices are 32-bit elements; how exact they have to be, the bound alone decides.
A program may use at most 64 MiB of HBM per device.

v0:
```python
import math
import jax
import jax.numpy as jnp
from jax import lax
from jax.sharding import PartitionSpec as P

CAP = 2
WAVENUMBER = 40.0
SOFTENING = 0.01


def far_terms(targets, sources, current):
    row_count = targets.shape[1]
    src_width = sources.shape[1]
    entry_limit = max(128, (1 << 20) // row_count)
    stride = math.gcd(src_width, 1 << entry_limit.bit_length() - 1)
    blocks = src_width // stride
    source_blocks = sources.reshape(3, blocks, stride).transpose(1, 0, 2)
    current_blocks = current.reshape(2, blocks, stride).transpose(1, 0, 2)

    def accumulate(running, block_pair):
        points, values = block_pair
        delta_x = targets[0][:, None] - points[0][None, :]
        delta_y = targets[1][:, None] - points[1][None, :]
        delta_z = targets[2][:, None] - points[2][None, :]
        distance = jnp.sqrt(
            delta_x * delta_x + delta_y * delta_y + delta_z * delta_z + SOFTENING * SOFTENING
        )
        phases = WAVENUMBER * distance
        kernel_re = jnp.cos(phases) / distance
        kernel_im = -jnp.sin(phases) / distance
        real_part = jnp.sum(kernel_re * values[0][None, :] - kernel_im * values[1][None, :], axis=1)
        imag_part = jnp.sum(kernel_re * values[1][None, :] + kernel_im * values[0][None, :], axis=1)
        return (running + jnp.stack([real_part, imag_part]), None)

    running, _ = lax.scan(
        accumulate, jnp.zeros((2, row_count), jnp.float32), (source_blocks, current_blocks)
    )
    return running


def far_part(test_points, src_points, currents):
    block_src, block_cur = (
        lax.all_gather(src_points, "row", axis=1, tiled=True),
        lax.all_gather(currents, "row", axis=1, tiled=True),
    )
    return far_terms(
        test_points,
        lax.all_gather(block_src, "col", axis=1, tiled=True),
        lax.all_gather(block_cur, "col", axis=1, tiled=True),
    )


def near_part(currents, near_blocks, near_dest, near_tile):
    items = near_blocks.shape[0]
    row_dev = near_blocks.shape[2]
    tile_width = near_blocks.shape[3]
    columns = lax.axis_size("col")
    tile_count = currents.shape[1] // tile_width
    highest = lax.Precision.HIGHEST
    tile_ids = near_tile[:, 0]
    target_col = near_dest[:, 0]
    picker = (tile_ids[:, None] == jnp.arange(tile_count, dtype=jnp.int32)[None, :]).astype(
        jnp.float32
    )
    chosen = jnp.einsum(
        "kt,ctj->kcj", picker, currents.reshape(2, tile_count, tile_width), precision=highest
    )
    blocks_re = near_blocks[:, 0]
    blocks_im = near_blocks[:, 1]
    term_re = jnp.einsum("kij,kj->ki", blocks_re, chosen[:, 0], precision=highest) - jnp.einsum(
        "kij,kj->ki", blocks_im, chosen[:, 1], precision=highest
    )
    term_im = jnp.einsum("kij,kj->ki", blocks_re, chosen[:, 1], precision=highest) + jnp.einsum(
        "kij,kj->ki", blocks_im, chosen[:, 0], precision=highest
    )
    terms = jnp.concatenate([term_re, term_im], axis=1)
    positions = jnp.arange(items, dtype=jnp.int32)
    earlier = (target_col[:, None] == target_col[None, :]) & (
        positions[None, :] < positions[:, None]
    )
    ranking = jnp.sum(earlier.astype(jnp.int32), axis=1)
    slot_ids = target_col * CAP + ranking
    placer = (slot_ids[:, None] == jnp.arange(columns * CAP, dtype=jnp.int32)[None, :]).astype(
        jnp.float32
    )
    outgoing = jnp.einsum("ks,kf->sf", placer, terms, precision=highest).reshape(
        columns, CAP * 2 * row_dev
    )
    incoming = lax.all_to_all(outgoing, "col", split_axis=0, concat_axis=0, tiled=True)
    return incoming.reshape(columns * CAP, 2, row_dev).sum(axis=0)


def local(test_points, src_points, currents, near_blocks, near_dest, near_tile):
    total_sources = src_points.shape[1] * lax.axis_size("row") * lax.axis_size("col")
    factor = 1.0 / math.sqrt(total_sources)
    far = far_part(test_points, src_points, currents)
    near = near_part(currents, near_blocks, near_dest, near_tile)
    return far * factor + near


def solution(mesh):
    in_specs = (
        P(None, ("row", "col")),
        P(None, ("row", "col")),
        P(None, ("row", "col")),
        P(("row", "col"), None, None, None),
        P(("row", "col"), None),
        P(("row", "col"), None),
    )
    out_specs = P(None, ("row", "col"))
    return jax.shard_map(local, mesh=mesh, in_specs=in_specs, out_specs=out_specs, check_vma=False)
```

profile of v0, /device:TPU:8, one launch (start us, length us, event | category | flops | bytes accessed | tf_op | source)
XLA Modules:
  0.0 363.5 jit_solution(17013263100812028713)
XLA Ops:
  6.5 0.0 all-gather.5.cloned.1.call-start
  6.5 6.6 %all_gather.14 = f32[2,4096]{1,0:T(2,128)} all-gather(f32[2,1024]{1,0:T(2,128)} %param.10), channel_id=1, replica_groups=mesh['row'=4,'col'=64] {'row'}, dimensions={1}, use_global_device_ids=true | all-gather | bytes 40960 | tf_op jit(solution)/shard_map/all_gather | solution.py:45
  13.1 0.0 all-gather.5.cloned.1.call-update
  13.1 0.0 all-gather.3.cloned.1.call-start
  13.2 5.9 %all_gather.12 = f32[3,4096]{1,0:T(4,128)} all-gather(f32[3,1024]{1,0:T(4,128)} %param.9), channel_id=1, replica_groups=mesh['row'=4,'col'=64] {'row'}, dimensions={1}, use_global_device_ids=true | all-gather | bytes 61440 | tf_op jit(solution)/shard_map/all_gather | solution.py:44
  19.1 0.0 all-gather.3.cloned.1.call-update
  19.1 0.9 fusion.18
  20.1 2.0 fusion.6
  22.1 2.0 fusion.2
  24.1 2.0 fusion.4
  26.1 2.0 fusion
  28.1 0.9 convert_reduce_fusion
  29.0 0.7 fusion.24
  29.7 0.3 fusion.12
  30.0 0.7 all_to_all.6
  30.7 14.4 %all-to-all-start = ((f32[64,1,64]{2,1,0:T(1,128)}), f32[64,1,64]{2,1,0:T(1,128)S(1)}, u32[]{:S(2)}, u32[]{:S(2)}) async-start(f32[64,1,64]{2,1,0:T(1,128)} %bitcast.27), calls=%async_computation | async-start | bytes 65536 | tf_op jit(solution)/shard_map/all_to_all | solution.py:90
  45.0 10.8 %all-to-all-done = f32[64,1,64]{2,1,0:T(1,128)S(1)} async-done(((f32[64,1,64]{2,1,0:T(1,128)}), f32[64,1,64]{2,1,0:T(1,128)S(1)}, u32[]{:S(2)}, u32[]{:S(2)}) %all-to-all-start) | async-done | bytes 16416 | tf_op jit(solution)/shard_map/all_to_all | solution.py:90
  55.8 0.5 broadcast.38
  56.3 0.7 reduce.3
  57.1 0.1 reshape.35
  57.2 0.1 reduce_sum.40
  57.4 77.2 %all-gather.5.cloned.1.call-done = f32[2,262144]{1,0:T(2,128)} async-done(((f32[2,4096]{1,0:T(2,128)}), f32[2,262144]{1,0:T(2,128)}) %all-gather.5.cloned.1.call-update) | async-done | bytes 2097168 | tf_op jit(solution)/shard_map/all_gather | solution.py:50
  134.6 127.7 %all-gather.3.cloned.1.call-done = f32[3,262144]{1,0:T(4,128)} async-done(((f32[3,4096]{1,0:T(4,128)}), f32[3,262144]{1,0:T(4,128)}) %all-gather.3.cloned.1.call-update) | async-done | bytes 3145744 | tf_op jit(solution)/shard_map/all_gather | solution.py:49
  262.3 93.8 %while.11 = (s32[]{:T(128)}, f32[2,16]{1,0:T(2,128)S(1)}, f32[3,16]{1,0:T(4,128)}, f32[4,3,65536]{2,1,0:T(4,128)}, f32[4,2,65536]{2,1,0:T(2,128)}, /*index=5*/s32[]{:T(128)}, s32[]{:T(128)}, s32[]{}, s32[]{}) while((s32[]{:T(128)}, f32[2,16]{1,0:T(2,128)S(1)}, f32[3,16]{1,0:T(4,128)}, f32[4,3,65536]{2,1,0:T(4,128)}, ...), condition=%wide.region_3.4_spmd.clone, body=%wide.region_0.3_spmd.clone.sunk | while | flops 22020164 | bytes 3933387 | solution.py:36
  262.3 3.4 constant_dynamic-slice_fusion.6
  265.7 0.8 slice_bitcast_fusion.4
  266.5 19.1 %subtract_reduce_fusion.2 = (f32[16]{0:T(128)S(1)}, f32[16]{0:T(128)S(1)}) fusion(f32[65536]{0:T(1024)S(1)} %bitcast.82, f32[65536]{0:T(1024)S(1)} %bitcast.81, f32[65536]{0:T(1024)S(1)} %bitcast.83, f32[16]{0:T(128)S(1)} %get-tuple-element.120, f32[65536]{0:T(1024)S(1)} %bitcast.84, f32[16]{0:T(128)S(1)} %get-tuple-element.122, ...), kind=kLoop, calls=%fused_computation.1.clone.1 | loop fusion | flops 22020064 | bytes 1311040 | tf_op jit(solution)/shard_map/while/body/eval_jaxpr/reduce_sum | solution.py:32
  285.6 3.7 %constant_dynamic-slice_fusion.6 = (f32[1,1,65536]{2,1,0:T(1,128)S(1)}, f32[1,1,65536]{2,1,0:T(1,128)S(1)}, f32[1,1,65536]{2,1,0:T(1,128)S(1)}, f32[1,1,65536]{2,1,0:T(1,128)S(1)}, f32[1,1,65536]{2,1,0:T(1,128)S(1)}) fusion(f32[4,2,65536]{2,1,0:T(2,128)} %get-tuple-element.149, s32[]{:T(128)} %get-tuple-element.136, s32[]{:T(128)S(6)} %add.101, ...), kind=kLoop, calls=%fused_computation.5.clone.1 | loop fusion | bytes 2621452 | tf_op jit(solution)/shard_map/while/body/eval_jaxpr/slice | solution.py:32
  289.3 0.8 slice_bitcast_fusion.4
  290.1 19.1 %subtract_reduce_fusion.2 = (f32[16]{0:T(128)S(1)}, f32[16]{0:T(128)S(1)}) fusion(f32[65536]{0:T(1024)S(1)} %bitcast.82, f32[65536]{0:T(1024)S(1)} %bitcast.81, f32[65536]{0:T(1024)S(1)} %bitcast.83, f32[16]{0:T(128)S(1)} %get-tuple-element.120, f32[65536]{0:T(1024)S(1)} %bitcast.84, f32[16]{0:T(128)S(1)} %get-tuple-element.122, ...), kind=kLoop, calls=%fused_computation.1.clone.1 | loop fusion | flops 22020064 | bytes 1311040 | tf_op jit(solution)/shard_map/while/body/eval_jaxpr/reduce_sum | solution.py:32
  309.2 3.5 constant_dynamic-slice_fusion.6
  312.7 0.8 slice_bitcast_fusion.4
  313.5 19.1 %subtract_reduce_fusion.2 = (f32[16]{0:T(128)S(1)}, f32[16]{0:T(128)S(1)}) fusion(f32[65536]{0:T(1024)S(1)} %bitcast.82, f32[65536]{0:T(1024)S(1)} %bitcast.81, f32[65536]{0:T(1024)S(1)} %bitcast.83, f32[16]{0:T(128)S(1)} %get-tuple-element.120, f32[65536]{0:T(1024)S(1)} %bitcast.84, f32[16]{0:T(128)S(1)} %get-tuple-element.122, ...), kind=kLoop, calls=%fused_computation.1.clone.1 | loop fusion | flops 22020064 | bytes 1311040 | tf_op jit(solution)/shard_map/while/body/eval_jaxpr/reduce_sum | solution.py:32
  332.7 3.6 constant_dynamic-slice_fusion.6
  336.2 0.8 slice_bitcast_fusion.4
  337.0 19.1 %subtract_reduce_fusion.2 = (f32[16]{0:T(128)S(1)}, f32[16]{0:T(128)S(1)}) fusion(f32[65536]{0:T(1024)S(1)} %bitcast.82, f32[65536]{0:T(1024)S(1)} %bitcast.81, f32[65536]{0:T(1024)S(1)} %bitcast.83, f32[16]{0:T(128)S(1)} %get-tuple-element.120, f32[65536]{0:T(1024)S(1)} %bitcast.84, f32[16]{0:T(128)S(1)} %get-tuple-element.122, ...), kind=kLoop, calls=%fused_computation.1.clone.1 | loop fusion | flops 22020064 | bytes 1311040 | tf_op jit(solution)/shard_map/while/body/eval_jaxpr/reduce_sum | solution.py:32
  356.1 0.6 multiply_add_fusion
  (8 shorter events, 0.1 us)
Async XLA Ops:
  6.5 128.1 %all-gather.5.cloned.1.call-start = ((), (), s32[]{:S(2)}) async-start(), calls=%async_computation.2 | async-start | bytes 2129920 | tf_op jit(solution)/shard_map/all_gather | solution.py:50
  13.1 249.2 %all-gather.3.cloned.1.call-start = ((), (), s32[]{:S(2)}) async-start(), calls=%async_computation.1 | async-start | bytes 4259840 | tf_op jit(solution)/shard_map/all_gather | solution.py:49
  30.7 25.2 %all-to-all-start = ((f32[64,1,64]{2,1,0:T(1,128)}), f32[64,1,64]{2,1,0:T(1,128)S(1)}, u32[]{:S(2)}, u32[]{:S(2)}) async-start(f32[64,1,64]{2,1,0:T(1,128)} %bitcast.27), calls=%async_computation | async-start | bytes 65536 | tf_op jit(solution)/shard_map/all_to_all | solution.py:90
Sparse Core Ops, SparseCore 0:
  13.3 121.3 all-gather.4
  138.1 124.1 all-gather.2
where the time goes:
time: 364 us
  waiting for transfers between devices  216 us (59%)
  other arithmetic  79.4 us (22%)
  local copies, waits for them, and re-layouts  18.7 us (5%)
  starting transfers between devices  14.4 us (4%)
  between operations  13.5 us (4%)
  blocking collectives  12.5 us (3%)
  matrix products  9.2 us (3%)
    all_gather x1, waiting for transfers between devices, far_part(): lax.all_gather(block_src, 'col', axis=1, tiled=True)  128 us
    all_gather x1, waiting for transfers between devices, far_part(): lax.all_gather(block_cur, 'col', axis=1, tiled=True)  77.2 us
    reduce_sum x4, other arithmetic, accumulate(): jnp.sum(kernel_re * values[0][None, :] - kernel_im * values[1][None, :],...  76.3 us
    all_to_all x1, starting transfers between devices, near_part(): lax.all_to_all(outgoing, 'col', split_axis=0, concat_axis=0, tiled=True)  14.4 us
    slice x4, local copies, waits for them, and re-layouts, accumulate(): values[0][None, :]  14.1 us
    all_to_all x1, waiting for transfers between devices, near_part(): lax.all_to_all(outgoing, 'col', split_axis=0, concat_axis=0, tiled=True)  10.8 us
  transfers between devices with their start and end apart: 3, of which 3 were waited for; matrix products, arithmetic and copies ran while one was open for 3% of the time, Pallas kernels for 0%

commit v1 on v0

--- a/solution.py
+++ b/solution.py
@@ -44,9 +44,17 @@
         lax.all_gather(src_points, "row", axis=1, tiled=True),
         lax.all_gather(currents, "row", axis=1, tiled=True),
     )
+
+    def connect_the_knots(z_in, row_axis):
+        new = jnp.concatenate(
+            lax.all_to_all(jnp.stack([z_in] * lax.axis_size(row_axis), axis=0), row_axis, 0, 0),
+            axis=1,
+        )
+        return new
+
     return far_terms(
         test_points,
-        lax.all_gather(block_src, "col", axis=1, tiled=True),
+        connect_the_knots(block_src, "col"),
         lax.all_gather(block_cur, "col", axis=1, tiled=True),
     )
 

time: 364 us -> 294 us (0.81)
  waiting for transfers between devices: 216 us -> 133 us
  starting transfers between devices: 14.4 us -> 22.2 us
  blocking collectives: 12.5 us -> 17.2 us
    all_gather x1 -> x0, waiting for transfers between devices: 128 us -> none  [far_part(): lax.all_gather(block_src, 'col', axis=1, tiled=True)]
    all_gather x1, waiting for transfers between devices: 77.2 us -> 128 us  [far_part(): lax.all_gather(block_cur, 'col', axis=1, tiled=True)]
    all_to_all x0 -> x1, starting transfers between devices: none -> 7.58 us  [connect_the_knots(): lax.all_to_all(jnp.stack([z_in] * lax.axis_size(row_axis), axis=0), row_a...]
    all_to_all x1, waiting for transfers between devices: 10.8 us -> 5.49 us  [near_part(): lax.all_to_all(outgoing, 'col', split_axis=0, concat_axis=0, tiled=True)]
    all_gather x1, blocking collectives: 6.57 us -> 11.7 us  [far_part(): lax.all_gather(currents, 'row', axis=1, tiled=True)]
  transfers between devices with their start and end apart: 3 -> 3, of which waited for: 3 -> 2; matrix products, arithmetic and copies ran while one was open for 3% -> 1% of each run, Pallas kernels for 0% -> 0%
where the time goes in v1:
time: 294 us; the launch traced here: 293 us
  waiting for transfers between devices  133 us (45%)
  other arithmetic  79.5 us (27%)
  starting transfers between devices  22.2 us (8%)
  local copies, waits for them, and re-layouts  18.4 us (6%)
  blocking collectives  17.2 us (6%)
  between operations  13.5 us (5%)
  matrix products  9.2 us (3%)
    all_gather x1, waiting for transfers between devices, far_part(): lax.all_gather(block_cur, 'col', axis=1, tiled=True)  128 us
    reduce_sum x4, other arithmetic, accumulate(): jnp.sum(kernel_re * values[0][None, :] - kernel_im * values[1][None, :],...  76.4 us
    all_to_all x1, starting transfers between devices, near_part(): lax.all_to_all(outgoing, 'col', split_axis=0, concat_axis=0, tiled=True)  14.6 us
    slice x4, local copies, waits for them, and re-layouts, accumulate(): values[0][None, :]  14 us
    all_gather x1, blocking collectives, far_part(): lax.all_gather(currents, 'row', axis=1, tiled=True)  11.7 us
    all_to_all x1, starting transfers between devices, connect_the_knots(): lax.all_to_all(jnp.stack([z_in] * lax.axis_size(row_axis), axis=0), row_a...  7.58 us
  transfers between devices with their start and end apart: 3, of which 2 were waited for; matrix products, arithmetic and copies ran while one was open for 1% of the time, Pallas kernels for 0%

profile of v1, /device:TPU:8, one launch (start us, length us, event | category | flops | bytes accessed | tf_op | source)
XLA Modules:
  0.0 293.1 jit_solution(14032323530267376620)
XLA Ops:
  6.5 0.9 fusion.18
  7.5 2.0 fusion.2
  9.5 2.0 fusion.4
  11.5 2.0 fusion.6
  13.5 2.0 fusion
  15.5 0.9 convert_reduce_fusion
  16.4 0.7 fusion.24
  17.0 0.3 fusion.12
  17.4 0.7 all_to_all.10
  18.0 14.6 %all-to-all-start.1 = ((f32[64,1,64]{2,1,0:T(1,128)}), f32[64,1,64]{2,1,0:T(1,128)S(1)}, u32[]{:S(2)}, u32[]{:S(2)}) async-start(f32[64,1,64]{2,1,0:T(1,128)} %bitcast.28), calls=%async_computation.1 | async-start | bytes 65536 | tf_op jit(solution)/shard_map/all_to_all | solution.py:98
  32.6 5.5 %all_gather.9 = f32[3,4096]{1,0:T(4,128)S(1)} all-gather(f32[3,1024]{1,0:T(4,128)} %param.9), channel_id=1, replica_groups=mesh['row'=4,'col'=64] {'row'}, dimensions={1}, use_global_device_ids=true | all-gather | bytes 61440 | tf_op jit(solution)/shard_map/all_gather | solution.py:44
  38.1 5.5 %all-to-all-done.1 = f32[64,1,64]{2,1,0:T(1,128)S(1)} async-done(((f32[64,1,64]{2,1,0:T(1,128)}), f32[64,1,64]{2,1,0:T(1,128)S(1)}, u32[]{:S(2)}, u32[]{:S(2)}) %all-to-all-start.1) | async-done | bytes 16416 | tf_op jit(solution)/shard_map/all_to_all | solution.py:98
  43.6 3.0 %stack.8 = f32[64,3,4096]{2,1,0:T(4,128)} broadcast(f32[3,4096]{1,0:T(4,128)S(1)} %all_gather.9), dimensions={1,2} | broadcast | bytes 3194880 | tf_op jit(solution)/shard_map/stack | solution.py:50
  46.6 0.0 copy-start
  46.6 0.0 copy-start.1
  46.6 7.6 %all-to-all-start = ((f32[64,3,4096]{2,1,0:T(4,128)}), f32[64,3,4096]{2,1,0:T(4,128)}, u32[]{:S(2)}, u32[]{:S(2)}) async-start(f32[64,3,4096]{2,1,0:T(4,128)} %stack.8), calls=%async_computation | async-start | bytes 8388608 | tf_op jit(solution)/shard_map/all_to_all | solution.py:50
  54.1 0.0 all-gather.2.cloned.1.call-start
  54.2 0.0 copy-done
  54.2 11.7 %all_gather.10 = f32[2,4096]{1,0:T(2,128)} all-gather(f32[2,1024]{1,0:T(2,128)S(1)} %copy-done), channel_id=1, replica_groups=mesh['row'=4,'col'=64] {'row'}, dimensions={1}, use_global_device_ids=true | all-gather | bytes 40960 | tf_op jit(solution)/shard_map/all_gather | solution.py:45
  65.9 0.0 all-gather.2.cloned.1.call-update
  65.9 0.5 broadcast.40
  66.5 0.7 reduce.3
  67.2 0.1 reshape.37
  67.4 0.1 reduce_sum.40
  67.5 127.6 %all-gather.2.cloned.1.call-done = f32[2,262144]{1,0:T(2,128)} async-done(((f32[2,4096]{1,0:T(2,128)}), f32[2,262144]{1,0:T(2,128)}) %all-gather.2.cloned.1.call-update) | async-done | bytes 2097168 | tf_op jit(solution)/shard_map/all_gather | solution.py:58
  195.1 0.0 all-to-all-done
  195.1 0.0 copy-done.1
  195.1 90.6 %while.11 = (s32[]{:T(128)}, f32[2,16]{1,0:T(2,128)S(1)}, f32[3,16]{1,0:T(4,128)S(1)}, f32[4,3,65536]{2,1,0:T(4,128)}, f32[4,2,65536]{2,1,0:T(2,128)}, /*index=5*/s32[]{:T(128)}, s32[]{:T(128)}, s32[]{}, s32[]{}) while((s32[]{:T(128)}, f32[2,16]{1,0:T(2,128)S(1)}, f32[3,16]{1,0:T(4,128)S(1)}, f32[4,3,65536]{2,1,0:T(4,128)}, ...), condition=%wide.region_3.4_spmd.clone, body=%wide.region_0.3_spmd.clone.sunk | while | flops 22020164 | bytes 3933387 | solution.py:36
  195.1 3.4 %constant_dynamic-slice_fusion.6 = (f32[1,1,65536]{2,1,0:T(1,128)S(1)}, f32[1,1,65536]{2,1,0:T(1,128)S(1)}, f32[1,1,65536]{2,1,0:T(1,128)S(1)}, f32[1,1,65536]{2,1,0:T(1,128)S(1)}, f32[1,1,65536]{2,1,0:T(1,128)S(1)}) fusion(f32[4,2,65536]{2,1,0:T(2,128)} %get-tuple-element.149, s32[]{:T(128)} %get-tuple-element.136, s32[]{:T(128)S(6)} %add.101, ...), kind=kLoop, calls=%fused_computation.5.clone.1 | loop fusion | bytes 2621452 | tf_op jit(solution)/shard_map/while/body/eval_jaxpr/slice | solution.py:32
  198.5 19.1 %subtract_reduce_fusion.2 = (f32[16]{0:T(128)S(1)}, f32[16]{0:T(128)S(1)}) fusion(f32[65536]{0:T(1024)S(1)} %bitcast.84, f32[65536]{0:T(1024)S(1)} %bitcast.83, f32[65536]{0:T(1024)S(1)} %bitcast.85, f32[16]{0:T(128)S(1)} %get-tuple-element.120, f32[65536]{0:T(1024)S(1)} %bitcast.86, f32[16]{0:T(128)S(1)} %get-tuple-element.122, ...), kind=kLoop, calls=%fused_computation.1.clone.1 | loop fusion | flops 22020064 | bytes 1311040 | tf_op jit(solution)/shard_map/while/body/eval_jaxpr/reduce_sum | solution.py:32
  217.6 3.6 %constant_dynamic-slice_fusion.6 = (f32[1,1,65536]{2,1,0:T(1,128)S(1)}, f32[1,1,65536]{2,1,0:T(1,128)S(1)}, f32[1,1,65536]{2,1,0:T(1,128)S(1)}, f32[1,1,65536]{2,1,0:T(1,128)S(1)}, f32[1,1,65536]{2,1,0:T(1,128)S(1)}) fusion(f32[4,2,65536]{2,1,0:T(2,128)} %get-tuple-element.149, s32[]{:T(128)} %get-tuple-element.136, s32[]{:T(128)S(6)} %add.101, ...), kind=kLoop, calls=%fused_computation.5.clone.1 | loop fusion | bytes 2621452 | tf_op jit(solution)/shard_map/while/body/eval_jaxpr/slice | solution.py:32
  221.2 19.1 %subtract_reduce_fusion.2 = (f32[16]{0:T(128)S(1)}, f32[16]{0:T(128)S(1)}) fusion(f32[65536]{0:T(1024)S(1)} %bitcast.84, f32[65536]{0:T(1024)S(1)} %bitcast.83, f32[65536]{0:T(1024)S(1)} %bitcast.85, f32[16]{0:T(128)S(1)} %get-tuple-element.120, f32[65536]{0:T(1024)S(1)} %bitcast.86, f32[16]{0:T(128)S(1)} %get-tuple-element.122, ...), kind=kLoop, calls=%fused_computation.1.clone.1 | loop fusion | flops 22020064 | bytes 1311040 | tf_op jit(solution)/shard_map/while/body/eval_jaxpr/reduce_sum | solution.py:32
  240.4 3.5 %constant_dynamic-slice_fusion.6 = (f32[1,1,65536]{2,1,0:T(1,128)S(1)}, f32[1,1,65536]{2,1,0:T(1,128)S(1)}, f32[1,1,65536]{2,1,0:T(1,128)S(1)}, f32[1,1,65536]{2,1,0:T(1,128)S(1)}, f32[1,1,65536]{2,1,0:T(1,128)S(1)}) fusion(f32[4,2,65536]{2,1,0:T(2,128)} %get-tuple-element.149, s32[]{:T(128)} %get-tuple-element.136, s32[]{:T(128)S(6)} %add.101, ...), kind=kLoop, calls=%fused_computation.5.clone.1 | loop fusion | bytes 2621452 | tf_op jit(solution)/shard_map/while/body/eval_jaxpr/slice | solution.py:32
  243.9 19.1 %subtract_reduce_fusion.2 = (f32[16]{0:T(128)S(1)}, f32[16]{0:T(128)S(1)}) fusion(f32[65536]{0:T(1024)S(1)} %bitcast.84, f32[65536]{0:T(1024)S(1)} %bitcast.83, f32[65536]{0:T(1024)S(1)} %bitcast.85, f32[16]{0:T(128)S(1)} %get-tuple-element.120, f32[65536]{0:T(1024)S(1)} %bitcast.86, f32[16]{0:T(128)S(1)} %get-tuple-element.122, ...), kind=kLoop, calls=%fused_computation.1.clone.1 | loop fusion | flops 22020064 | bytes 1311040 | tf_op jit(solution)/shard_map/while/body/eval_jaxpr/reduce_sum | solution.py:32
  263.1 3.5 %constant_dynamic-slice_fusion.6 = (f32[1,1,65536]{2,1,0:T(1,128)S(1)}, f32[1,1,65536]{2,1,0:T(1,128)S(1)}, f32[1,1,65536]{2,1,0:T(1,128)S(1)}, f32[1,1,65536]{2,1,0:T(1,128)S(1)}, f32[1,1,65536]{2,1,0:T(1,128)S(1)}) fusion(f32[4,2,65536]{2,1,0:T(2,128)} %get-tuple-element.149, s32[]{:T(128)} %get-tuple-element.136, s32[]{:T(128)S(6)} %add.101, ...), kind=kLoop, calls=%fused_computation.5.clone.1 | loop fusion | bytes 2621452 | tf_op jit(solution)/shard_map/while/body/eval_jaxpr/slice | solution.py:32
  266.6 19.1 %subtract_reduce_fusion.2 = (f32[16]{0:T(128)S(1)}, f32[16]{0:T(128)S(1)}) fusion(f32[65536]{0:T(1024)S(1)} %bitcast.84, f32[65536]{0:T(1024)S(1)} %bitcast.83, f32[65536]{0:T(1024)S(1)} %bitcast.85, f32[16]{0:T(128)S(1)} %get-tuple-element.120, f32[65536]{0:T(1024)S(1)} %bitcast.86, f32[16]{0:T(128)S(1)} %get-tuple-element.122, ...), kind=kLoop, calls=%fused_computation.1.clone.1 | loop fusion | flops 22020064 | bytes 1311040 | tf_op jit(solution)/shard_map/while/body/eval_jaxpr/reduce_sum | solution.py:32
  285.7 0.6 multiply_add_fusion
  (12 shorter events, 0.1 us)
Async XLA Ops:
  18.0 25.5 %all-to-all-start.1 = ((f32[64,1,64]{2,1,0:T(1,128)}), f32[64,1,64]{2,1,0:T(1,128)S(1)}, u32[]{:S(2)}, u32[]{:S(2)}) async-start(f32[64,1,64]{2,1,0:T(1,128)} %bitcast.28), calls=%async_computation.1 | async-start | bytes 65536 | tf_op jit(solution)/shard_map/all_to_all | solution.py:98
  46.6 7.6 %copy-start = (f32[2,1024]{1,0:T(2,128)S(1)}, f32[2,1024]{1,0:T(2,128)}, u32[]{:S(2)}) copy-start(f32[2,1024]{1,0:T(2,128)} %param.10) | copy-start | bytes 24580
  46.6 148.5 %copy-start.1 = (f32[3,16]{1,0:T(4,128)S(1)}, f32[3,16]{1,0:T(4,128)}, u32[]{:S(2)}) copy-start(f32[3,16]{1,0:T(4,128)} %param.8) | copy-start | bytes 580
  46.6 148.5 %all-to-all-start = ((f32[64,3,4096]{2,1,0:T(4,128)}), f32[64,3,4096]{2,1,0:T(4,128)}, u32[]{:S(2)}, u32[]{:S(2)}) async-start(f32[64,3,4096]{2,1,0:T(4,128)} %stack.8), calls=%async_computation | async-start | bytes 8388608 | tf_op jit(solution)/shard_map/all_to_all | solution.py:50
  54.1 140.9 %all-gather.2.cloned.1.call-start = ((), (), s32[]{:S(2)}) async-start(), calls=%async_computation.2 | async-start | bytes 2129920 | tf_op jit(solution)/shard_map/all_gather | solution.py:58
Sparse Core Ops, SparseCore 0:
  66.1 128.9 all-gather.1
